TPU v7x, 32 devices: a whole 2x2x4 slice. The times are simulated.
32 devices in a mesh: section: 4 (over y, x), dp: 8 (over z, core).
Axes of the slice: x: 2, y: 2, z: 4, core: 2. Of those that a mesh axis runs over, the one named last changes fastest.
Arguments:
- latents: bfloat16 [2048, 1536], P('dp'), may hold values from -6 to 6
- media: bfloat16 [8192, 1536], P('dp'), may hold values from -6 to 6
- segment_ids: int32 [8, 1024], P('dp'), may hold values from -1 to 3, as said below
- slot_map: int32 [8, 4], P('dp'), may hold values from 0 to 3, each once within a row
- gains: float32 [2, 3, 1536], P(None, None, ('section', 'dp')), may hold values from 0.5 to 1.5
- w_query: bfloat16 [4, 1536, 768], P('section', 'dp'), may hold values from -0.15625 to 0.15625
- w_key: bfloat16 [4, 1536, 768], P('section', 'dp'), may hold values from -0.15625 to 0.15625
- w_value: bfloat16 [4, 1536, 768], P('section', 'dp'), may hold values from -0.15625 to 0.15625
- w_out: bfloat16 [4, 768, 1536], P('section', 'dp'), may hold values from -1.25 to 1.25
- w_up: bfloat16 [4, 1536, 3072], P('section', 'dp'), may hold values from -0.15625 to 0.15625
- w_down: bfloat16 [4, 3072, 1536], P('section', 'dp'), may hold values from -0.078125 to 0.078125
- cotangent: bfloat16 [2048, 1536], P('dp'), may hold values from -6 to 6
Outputs:
- latents_out: float32 [2048, 1536], P('dp', 'section')
- latent_grad: float32 [2048, 1536], P('dp', 'section')
- media_grad: float32 [8192, 1536], P('dp')
- gain_grad: float32 [2, 3, 1536], P(None, None, ('section', 'dp'))
- query_grad: float32 [4, 1536, 768], P('section', 'dp')
- key_grad: float32 [4, 1536, 768], P('section', 'dp')
- value_grad: float32 [4, 1536, 768], P('section', 'dp')
- out_grad: float32 [4, 768, 1536], P('section', 'dp')
- up_grad: float32 [4, 1536, 3072], P('section', 'dp')
- down_grad: float32 [4, 3072, 1536], P('section', 'dp')
Inputs may be any that keep to these rules, and one draw needn't show every extreme that they name: `segment_ids`: in each sequence, images 0 to 3 each hold one run of one or more consecutive rows, in that order, and one or more pad rows (-1) follow them. `slot_map`: each row is a permutation of 0 to 3.
All inputs are finite; a program needn't handle non-finite values.
Results may differ from a plain program's by a relative error of at most 0.024.
Values may be sent and summed in bfloat16 or wider, within the bound.
No kernel may reach another device: no remote copies, remote signals or barrier semaphores. Data moves between devices by JAX's collectives and lax.ppermute only.
A program may use at most 256 MiB of HBM per device.

v0:
```python
import math
import jax
import jax.numpy as jnp
from jax import lax
from jax.sharding import PartitionSpec as P

HEAD_DIM = 96
LATENTS = 64
LAYERS = 2
HALF_HEADS = 8
epsilon = 1e-05
low = jnp.bfloat16
full = jnp.float32


def unit_rows(values):
    centered = values - jnp.mean(values, axis=-1, keepdims=True)
    variance = jnp.mean(centered * centered, axis=-1, keepdims=True)
    inverse = lax.rsqrt(variance + epsilon)
    return (centered * inverse, inverse)


def norm_back(unit, inverse, scaled):
    first = jnp.mean(scaled, axis=-1, keepdims=True)
    second = jnp.mean(scaled * unit, axis=-1, keepdims=True)
    return (scaled - first - unit * second) * inverse


def gelu_exact(values):
    return jax.nn.gelu(values, approximate=False)


def matmul(left, right):
    return jnp.dot(left, right, preferred_element_type=full)


def matmul_nt(left, right):
    return lax.dot_general(left, right, (((1,), (1,)), ((), ())), preferred_element_type=full)


def matmul_tn(left, right):
    return lax.dot_general(left, right, (((0,), (0,)), ((), ())), preferred_element_type=full)


def attend_forward(query_heads, key_heads, value_heads, allowed, score_scale):
    scores = jnp.einsum("qhd,khd->hqk", query_heads, key_heads, preferred_element_type=full)
    scores = jnp.where(allowed, scores * score_scale, -1e30)
    row_max = jnp.max(scores, axis=-1, keepdims=True)
    exponent = jnp.exp(scores - row_max)
    row_total = jnp.sum(exponent, axis=-1, keepdims=True)
    weights_low = (exponent / row_total).astype(low)
    attended = jnp.einsum("hqk,khd->qhd", weights_low, value_heads, preferred_element_type=full)
    return (attended, row_max + jnp.log(row_total))


def attend_backward(
    query_heads, key_heads, value_heads, allowed, score_scale, log_total, grad_heads
):
    scores = jnp.einsum("qhd,khd->hqk", query_heads, key_heads, preferred_element_type=full)
    scores = jnp.where(allowed, scores * score_scale, -1e30)
    weights_full = jnp.exp(scores - log_total)
    weights_low = weights_full.astype(low)
    grad_value = jnp.einsum("hqk,qhd->khd", weights_low, grad_heads, preferred_element_type=full)
    grad_weights = jnp.einsum("qhd,khd->hqk", grad_heads, value_heads, preferred_element_type=full)
    row_inner = jnp.sum(weights_full * grad_weights, axis=-1, keepdims=True)
    grad_scores = (weights_full * (grad_weights - row_inner)).astype(low)
    grad_query = (
        jnp.einsum("hqk,khd->qhd", grad_scores, key_heads, preferred_element_type=full)
        * score_scale
    )
    grad_key = (
        jnp.einsum("hqk,qhd->khd", grad_scores, query_heads, preferred_element_type=full)
        * score_scale
    )
    return (grad_query, grad_key, grad_value)


def per_device(
    latents,
    media,
    segment_ids,
    slot_map,
    gains,
    w_query,
    w_key,
    w_value,
    w_out,
    w_up,
    w_down,
    cotangent,
):
    section = lax.axis_index("section")
    section_count = lax.axis_size("section")
    dp_index = lax.axis_index("dp")
    dp_count = lax.axis_size("dp")
    layer_bit = section // 2
    on_first = layer_bit == 0
    stride = dp_count // HALF_HEADS
    row_bit = dp_index // stride % 2
    row_first = row_bit == 0
    seq_rows = segment_ids.shape[1]
    slot_count = slot_map.shape[1]
    feature_width = latents.shape[1]
    latent_rows = latents.shape[0]
    heads = HALF_HEADS // 2
    inner = heads * HEAD_DIM
    score_scale = 1.0 / math.sqrt(HEAD_DIM)

    def pick(first, second):
        return (jnp.where(on_first, first, second), jnp.where(on_first, second, first))

    def swap_layer(value):
        pairs = [(source, source ^ 2) for source in range(section_count)]
        return lax.ppermute(value, "section", pairs)

    def with_bit(index, bit):
        high, lowest = (index // (2 * stride), index % stride)
        return (2 * high + bit) * stride + lowest

    def bit_of(index):
        return index // stride % 2

    def turn_pairs(flip, back):
        pairs = []
        for source in range(section_count):
            for index in range(dp_count):
                layer, half = divmod(source, 2)
                target = (bit_of(index) * 2 + half) * dp_count + with_bit(index, layer ^ flip)
                pair = (source * dp_count + index, target)
                pairs.append(pair[::-1] if back else pair)
        return pairs

    def column_parts(weight, block):
        rows, width = weight.shape
        split = weight.reshape(rows, width // (2 * block), 2, block)
        return (split[:, :, 0].reshape(rows, -1), split[:, :, 1].reshape(rows, -1))

    def exchange_columns(even, odd):
        own, other = pick(even, odd)
        return pick(own, swap_layer(other))

    def join_columns(first, second, block):
        own, other = pick(first, second)
        even, odd = pick(own, swap_layer(other))
        rows, width = even.shape
        pieces = [part.reshape(rows, width // block, 1, block) for part in (even, odd)]
        return jnp.concatenate(pieces, axis=2).reshape(rows, 2 * width).astype(full)

    def exchange_rows(weight):
        half = weight.shape[0] // 2
        near, far = pick(weight[:half], weight[half:])
        first = lax.ppermute(near, ("section", "dp"), turn_pairs(0, False))
        second = lax.ppermute(far, ("section", "dp"), turn_pairs(1, False))
        return (jnp.where(row_first, first, second), jnp.where(row_first, second, first))

    def join_rows(first, second):
        near = jnp.where(row_first, first, second)
        far = jnp.where(row_first, second, first)
        near = lax.ppermute(near, ("section", "dp"), turn_pairs(0, True))
        far = lax.ppermute(far, ("section", "dp"), turn_pairs(1, True))
        return jnp.concatenate(pick(near, far), axis=0).astype(full)

    def gather_rows(piece):
        gathered = lax.all_gather(piece, "dp", axis=0, tiled=True)
        if stride > 1:
            width = gathered.shape[1]
            gathered = gathered.reshape(-1, 2, stride, piece.shape[0], width)
            gathered = gathered.transpose(0, 2, 1, 3, 4).reshape(-1, width)
        return gathered

    def scatter_rows(grad):
        if stride > 1:
            width = grad.shape[1]
            piece = grad.shape[0] // dp_count
            grad = grad.reshape(-1, stride, 2, piece, width)
            grad = grad.transpose(0, 2, 1, 3, 4).reshape(-1, width)
        return lax.psum_scatter(grad.astype(low), "dp", scatter_dimension=0, tiled=True)

    def scatter_columns(grad):
        return lax.psum_scatter(grad.astype(low), "dp", scatter_dimension=0, tiled=True)

    def sum_to_slots(partial):
        blocks = partial.astype(low).reshape(section_count, -1, feature_width)
        arrived = lax.all_to_all(blocks, "section", split_axis=0, concat_axis=0)
        return jnp.sum(arrived.astype(full), axis=0)

    def from_slots(rows):
        return lax.all_gather(rows, "section", axis=0, tiled=True)

    def to_columns(rows):
        moved = lax.all_to_all(rows.astype(low), "section", split_axis=1, concat_axis=0, tiled=True)
        return moved.astype(full)

    query_parts = column_parts(w_query[0], HEAD_DIM)
    key_parts = column_parts(w_key[0], HEAD_DIM)
    value_parts = column_parts(w_value[0], HEAD_DIM)
    joined = [
        jnp.concatenate([query_parts[i], key_parts[i], value_parts[i]], axis=1) for i in range(2)
    ]
    qkv_pieces = exchange_columns(joined[0], joined[1])
    out_pieces = exchange_rows(w_out[0])
    hidden_block = w_up.shape[2] // HALF_HEADS
    up_pieces = exchange_columns(*column_parts(w_up[0], hidden_block))
    down_pieces = exchange_rows(w_down[0])
    qkv_w, out_w, up_w, down_w = ([], [], [], [])
    for layer in range(LAYERS):
        qkv_w.append(lax.all_gather(qkv_pieces[layer], "dp", axis=0, tiled=True))
        out_w.append(gather_rows(out_pieces[layer]))
        up_w.append(lax.all_gather(up_pieces[layer], "dp", axis=0, tiled=True))
        down_w.append(gather_rows(down_pieces[layer]))
    query_w = [weight[:, :inner] for weight in qkv_w]
    key_w = [weight[:, inner : 2 * inner] for weight in qkv_w]
    value_w = [weight[:, 2 * inner :] for weight in qkv_w]
    all_gains = lax.all_gather(gains, ("section", "dp"), axis=2, tiled=True)
    image_hot = segment_ids[:, :, None] == jnp.arange(slot_count, dtype=jnp.int32)[None, None, :]
    media_slot = jnp.sum(jnp.where(image_hot, slot_map[:, None, :], 0), axis=2) - (
        segment_ids < 0
    ).astype(jnp.int32)
    media_unit, media_inverse = unit_rows(media.astype(full))
    latent_slot = jnp.arange(latent_rows, dtype=jnp.int32) // LATENTS
    key_slot = jnp.concatenate([media_slot[0], latent_slot])
    allowed = latent_slot[None, :, None] == key_slot[None, None, :]

    def split_heads(rows):
        return rows.reshape(rows.shape[0], heads, HEAD_DIM)

    media_low = []
    media_key = []
    media_value = []
    for layer in range(LAYERS):
        media_low.append((media_unit * all_gains[layer, 0]).astype(low))
        media_key.append(matmul(media_low[layer], key_w[layer]).astype(low))
        media_value.append(matmul(media_low[layer], value_w[layer]).astype(low))
    saved = []
    slot_rows = latent_rows // section_count
    current = lax.dynamic_slice_in_dim(latents, section * slot_rows, slot_rows, 0).astype(full)
    for layer in range(LAYERS):
        unit_in, inverse_in = unit_rows(current)
        if layer == 0:
            whole_unit = unit_rows(latents.astype(full))[0]
            latent_low = (whole_unit * all_gains[layer, 1]).astype(low)
        else:
            latent_low = from_slots((unit_in * all_gains[layer, 1]).astype(low))
        projected = matmul(latent_low, qkv_w[layer]).astype(low)
        query_low = projected[:, :inner]
        key_heads = split_heads(
            jnp.concatenate([media_key[layer], projected[:, inner : 2 * inner]], axis=0)
        )
        value_heads = split_heads(
            jnp.concatenate([media_value[layer], projected[:, 2 * inner :]], axis=0)
        )
        query_heads = split_heads(query_low)
        attended, log_total = attend_forward(
            query_heads, key_heads, value_heads, allowed, score_scale
        )
        attended_low = attended.reshape(-1, inner).astype(low)
        middle = current + sum_to_slots(matmul(attended_low, out_w[layer]))
        unit_mid, inverse_mid = unit_rows(middle)
        ffn_low = from_slots((unit_mid * all_gains[layer, 2]).astype(low))
        hidden_pre = matmul(ffn_low, up_w[layer])
        active_low = gelu_exact(hidden_pre).astype(low)
        current = middle + sum_to_slots(matmul(active_low, down_w[layer]))
        saved.append(
            (
                unit_in,
                inverse_in,
                latent_low,
                query_heads,
                key_heads,
                value_heads,
                log_total,
                attended_low,
                unit_mid,
                inverse_mid,
                ffn_low,
                hidden_pre,
                active_low,
            )
        )
    latents_out = to_columns(current)
    gain_rows = [None] * LAYERS
    media_scaled = None
    pieces = [None] * LAYERS
    grad_low = cotangent
    grad_rows = lax.dynamic_slice_in_dim(cotangent, section * slot_rows, slot_rows, 0).astype(full)
    for layer in (1, 0):
        (
            unit_in,
            inverse_in,
            latent_low,
            query_heads,
            key_heads,
            value_heads,
            log_total,
            attended_low,
            unit_mid,
            inverse_mid,
            ffn_low,
            hidden_pre,
            active_low,
        ) = saved[layer]
        grad_active = matmul_nt(grad_low, down_w[layer])
        grad_hidden = jax.vjp(gelu_exact, hidden_pre)[1](grad_active)[0].astype(low)
        down_piece = scatter_rows(matmul_tn(active_low, grad_low))
        up_piece = scatter_columns(matmul_tn(ffn_low, grad_hidden))
        ffn_grad = sum_to_slots(matmul_nt(grad_hidden, up_w[layer]))
        gain_ffn_grad = jnp.sum(ffn_grad * unit_mid, axis=0)
        grad_middle = grad_rows + norm_back(unit_mid, inverse_mid, ffn_grad * all_gains[layer, 2])
        middle_low = from_slots(grad_middle.astype(low))
        grad_heads = split_heads(matmul_nt(middle_low, out_w[layer]).astype(low))
        out_piece = scatter_rows(matmul_tn(attended_low, middle_low))
        grad_query, grad_key, grad_value = attend_backward(
            query_heads, key_heads, value_heads, allowed, score_scale, log_total, grad_heads
        )
        grad_query = grad_query.reshape(-1, inner).astype(low)
        grad_key = grad_key.reshape(-1, inner).astype(low)
        grad_value = grad_value.reshape(-1, inner).astype(low)
        latent_part = (
            matmul_nt(grad_query, query_w[layer])
            + matmul_nt(grad_key[seq_rows:], key_w[layer])
            + matmul_nt(grad_value[seq_rows:], value_w[layer])
        )
        latent_grad_rows = sum_to_slots(latent_part)
        gain_latent_grad = jnp.sum(latent_grad_rows * unit_in, axis=0)
        grad_rows = grad_middle + norm_back(
            unit_in, inverse_in, latent_grad_rows * all_gains[layer, 1]
        )
        if layer > 0:
            grad_low = from_slots(grad_rows.astype(low))
        both_low = jnp.concatenate([media_low[layer], latent_low], axis=0)
        query_grad = matmul_tn(latent_low, grad_query)
        key_grad = matmul_tn(both_low, grad_key)
        value_grad = matmul_tn(both_low, grad_value)
        qkv_piece = scatter_columns(
            jnp.concatenate(
                [query_grad.astype(low), key_grad.astype(low), value_grad.astype(low)], axis=1
            )
        )
        media_part = matmul_nt(grad_key[:seq_rows], key_w[layer]) + matmul_nt(
            grad_value[:seq_rows], value_w[layer]
        )
        gain_media_grad = jnp.sum(media_part * media_unit, axis=0)
        scaled = media_part * all_gains[layer, 0]
        media_scaled = scaled if media_scaled is None else media_scaled + scaled
        gain_rows[layer] = jnp.stack([gain_media_grad, gain_latent_grad, gain_ffn_grad])
        pieces[layer] = (qkv_piece, out_piece, up_piece, down_piece)
    latent_grad = to_columns(grad_rows)
    media_grad = lax.psum(
        norm_back(media_unit, media_inverse, media_scaled).astype(low), "section"
    ).astype(full)
    gain_grad = lax.psum_scatter(
        jnp.stack(gain_rows), ("section", "dp"), scatter_dimension=2, tiled=True
    )
    qkv_grads = [
        join_columns(
            pieces[0][0][:, i * inner : (i + 1) * inner],
            pieces[1][0][:, i * inner : (i + 1) * inner],
            HEAD_DIM,
        )
        for i in range(3)
    ]
    out_grad = join_rows(pieces[0][1], pieces[1][1])
    up_grad = join_columns(pieces[0][2], pieces[1][2], hidden_block)
    down_grad = join_rows(pieces[0][3], pieces[1][3])
    return (
        latents_out,
        latent_grad,
        media_grad,
        gain_grad,
        qkv_grads[0][None],
        qkv_grads[1][None],
        qkv_grads[2][None],
        out_grad[None],
        up_grad[None],
        down_grad[None],
    )


def solution(mesh):
    placed = (
        P("dp", None),
        P("dp", None),
        P("dp", None),
        P("dp", None),
        P(None, None, ("section", "dp")),
        P("section", "dp", None),
        P("section", "dp", None),
        P("section", "dp", None),
        P("section", "dp", None),
        P("section", "dp", None),
        P("section", "dp", None),
        P("dp", None),
    )
    return jax.shard_map(
        per_device,
        mesh=mesh,
        in_specs=placed,
        out_specs=(
            P("dp", "section"),
            P("dp", "section"),
            P("dp", None),
            P(None, None, ("section", "dp")),
            P("section", "dp", None),
            P("section", "dp", None),
            P("section", "dp", None),
            P("section", "dp", None),
            P("section", "dp", None),
            P("section", "dp", None),
        ),
        check_vma=False,
    )
```

profile of v0, /device:TPU:1, one launch (start us, length us, event | category | flops | bytes accessed | tf_op | source)
XLA Modules:
  0.0 1105.7 jit_solution(2299678862208931435)
XLA Ops:
  20.2 9.9 collective-permute-done
  32.3 3.6 collective-permute-start.1
  43.5 14.9 %collective-permute-done.3 = bf16[192,1536]{1,0:T(8,128)(2,1)S(1)} collective-permute-done((bf16[192,1536]{1,0:T(8,128)(2,1)S(1)}, bf16[192,1536]{1,0:T(8,128)(2,1)S(1)}, u32[]{:S(2)}, u32[]{:S(2)}) %collective-permute-start.3) | collective-permute-done | bytes 589856 | tf_op jit(solution)/shard_map/ppermute | solution.py:114
  59.7 4.4 collective-permute-start.4
  66.5 9.5 collective-permute-done.4
  78.4 56.3 %all_gather.45 = f32[2,3,1536]{1,0,2:T(2,128)} all-gather(f32[2,3,48]{1,0,2:T(2,128)S(1)} %copy.170), channel_id=1, replica_groups=mesh['section'=4,'dp'=8] {'section','dp'}, dimensions={2}, use_global_device_ids=true | all-gather | bytes 38016 | tf_op jit(solution)/shard_map/all_gather | solution.py:214
  139.7 25.7 %slice_reduce_fusion = (f32[1536]{0:T(1024)S(1)}, f32[1536]{0:T(1024)S(1)}, f32[1536]{0:T(1024)S(1)}, f32[1536]{0:T(1024)S(1)}, f32[1536]{0:T(1024)S(1)}, /*index=5*/f32[1536]{0:T(1024)S(1)}) fusion(f32[2,3,1536]{1,0,2:T(2,128)S(1)} %copy-done.4), kind=kLoop, calls=%fused_computation.166 | loop fusion | bytes 73728 | tf_op jit(solution)/shard_map/slice | solution.py:259
  170.2 3.6 convolution_convert_fusion.15
  180.2 4.0 convolution_convert_fusion.25
  199.2 10.1 all-to-all-done
  210.0 9.0 all_gather.48
  219.0 8.8 multiply_convert_fusion.3
  227.8 4.9 convolution_convert_fusion.21
  236.3 17.8 %all-gather.17.cloned.1.call-done = bf16[1536,1152]{1,0:T(8,128)(2,1)} async-done(((bf16[192,1152]{1,0:T(8,128)(2,1)}), bf16[1536,1152]{1,0:T(8,128)(2,1)}) %all-gather.17.cloned.1.call-update) | async-done | bytes 3538960 | tf_op jit(solution)/shard_map/all_gather | solution.py:207
  254.1 5.1 convolution_convert_fusion.22
  259.2 4.0 convolution_convert_fusion.23
  263.8 11.0 all_gather.52
  298.6 10.3 all-to-all-done.2
  309.5 9.9 all_gather.54
  319.4 11.5 %all-gather.21.cloned.1.call-done = bf16[1536,1536]{1,0:T(8,128)(2,1)} async-done(((bf16[192,1536]{1,0:T(8,128)(2,1)}), bf16[1536,1536]{1,0:T(8,128)(2,1)}) %all-gather.21.cloned.1.call-update) | async-done | bytes 4718608 | tf_op jit(solution)/shard_map/all_gather | solution.py:209
  330.9 8.4 multiply_convert_fusion.2
  339.3 44.4 %all-gather.23.cloned.1.call-done = bf16[1536,1536]{1,0:T(8,128)(2,1)} async-done(((bf16[192,1536]{1,0:T(8,128)(2,1)}), bf16[1536,1536]{1,0:T(8,128)(2,1)}) %all-gather.23.cloned.1.call-update) | async-done | bytes 4718608 | tf_op jit(solution)/shard_map/all_gather | solution.py:164
  383.7 7.8 add_convert_fusion.1
  393.9 4.2 all-to-all-start.5
  398.1 4.8 convolution_convert_fusion.20
  402.9 5.9 all-to-all-done.5
  408.8 4.2 all-to-all-start.3
  414.6 8.8 all-to-all-done.3
  426.7 9.1 all_gather.57
  437.4 3.7 convolution_convert_fusion.9
  452.1 4.3 all-to-all-start.6
  459.4 5.8 fusion.60
  467.8 9.7 all_gather.58
  477.6 4.4 add_convert_fusion
  484.4 4.7 all-to-all-start.7
  489.1 7.8 convolution_add_fusion.1
  499.5 9.9 all_gather.59
  511.8 3.9 multiply_reduce_fusion
  526.2 4.3 all-to-all-start.8
  536.0 8.7 fusion.91
  553.7 5.1 fusion.13
  560.5 3.7 convolution_convert_fusion.4
  566.2 3.8 copy.202
  571.7 3.7 convolution_convert_fusion.6
  577.4 3.9 copy.200
  582.6 3.6 convolution_convert_fusion.2
  587.6 3.6 convolution_convert_fusion.3
  592.6 3.7 convolution_convert_fusion
  597.6 3.6 convolution_convert_fusion.1
  602.8 3.5 all-to-all-start.4
  613.8 14.0 %collective-permute-start.9 = (bf16[48,1536]{1,0:T(8,128)(2,1)S(1)}, bf16[48,1536]{1,0:T(8,128)(2,1)S(1)}, u32[]{:S(2)}, u32[]{:S(2)}) collective-permute-start(bf16[48,1536]{1,0:T(8,128)(2,1)S(1)} %get-tuple-element.155), channel_id=1, source_target_pairs={{0,0},{16,1},{2,2},{18,3},{4,4},{20,5},{6,6},{22,7},{8,8},{24,9},{... | collective-permute-start | bytes 442376 | tf_op jit(solution)/shard_map/ppermute | solution.py:159
  628.6 42.5 %reduce-scatter.28.cloned.1.call-done = f32[48,6]{1,0:T(8,128)} async-done(((f32[1536,6]{1,0:T(8,128)}), f32[48,6]{1,0:T(8,128)}) %reduce-scatter.28.cloned.1.call-update) | async-done | bytes 1168
  674.3 87.7 %all-reduce.2.cloned.1.call-done = bf16[1024,1536]{1,0:T(8,128)(2,1)} async-done(((bf16[1024,1536]{1,0:T(8,128)(2,1)}), bf16[1024,1536]{1,0:T(8,128)(2,1)}) %all-reduce.2.cloned.1.call-update) | async-done | bytes 3145744 | tf_op jit(solution)/shard_map/psum | solution.py:348
  762.0 5.5 convert_element_type.431
  767.4 38.7 %reduce-scatter.32.cloned.1.call-done = bf16[192,1152]{1,0:T(8,128)(2,1)} async-done(((bf16[1536,1152]{1,0:T(8,128)(2,1)}), bf16[192,1152]{1,0:T(8,128)(2,1)}) %reduce-scatter.32.cloned.1.call-update) | async-done | bytes 442384
  807.7 43.0 %reduce-scatter.30.cloned.1.call-done = bf16[192,1152]{1,0:T(8,128)(2,1)} async-done(((bf16[1536,1152]{1,0:T(8,128)(2,1)}), bf16[192,1152]{1,0:T(8,128)(2,1)}) %reduce-scatter.30.cloned.1.call-update) | async-done | bytes 442384
  855.1 4.9 collective-permute-done.7
  860.1 4.3 collective-permute-done.6
  864.7 41.7 %reduce-scatter.22.cloned.1.call-done = bf16[192,1536]{1,0:T(8,128)(2,1)} async-done(((bf16[1536,1536]{1,0:T(8,128)(2,1)}), bf16[192,1536]{1,0:T(8,128)(2,1)}) %reduce-scatter.22.cloned.1.call-update) | async-done | bytes 589840 | tf_op jit(solution)/shard_map/reduce_scatter | solution.py:180
  906.4 55.6 %reduce-scatter.20.cloned.1.call-done = bf16[192,1536]{1,0:T(8,128)(2,1)} async-done(((bf16[1536,1536]{1,0:T(8,128)(2,1)}), bf16[192,1536]{1,0:T(8,128)(2,1)}) %reduce-scatter.20.cloned.1.call-update) | async-done | bytes 589840 | tf_op jit(solution)/shard_map/reduce_scatter | solution.py:180
  972.6 45.0 %reduce-scatter.26.cloned.1.call-done = bf16[192,1536]{1,0:T(8,128)(2,1)} async-done(((bf16[1536,1536]{1,0:T(8,128)(2,1)}), bf16[192,1536]{1,0:T(8,128)(2,1)}) %reduce-scatter.26.cloned.1.call-update) | async-done | bytes 589840 | tf_op jit(solution)/shard_map/reduce_scatter | solution.py:177
  1017.6 55.6 %reduce-scatter.24.cloned.1.call-done = bf16[192,1536]{1,0:T(8,128)(2,1)} async-done(((bf16[1536,1536]{1,0:T(8,128)(2,1)}), bf16[192,1536]{1,0:T(8,128)(2,1)}) %reduce-scatter.24.cloned.1.call-update) | async-done | bytes 589840 | tf_op jit(solution)/shard_map/reduce_scatter | solution.py:177
  1075.6 5.8 collective-permute-start.12
  1087.9 6.3 collective-permute-done.12
  (459 shorter events, 201.0 us)
Async XLA Ops:
  7.2 163.0 %all-gather.9.cloned.1.call-start = ((), (), s32[]{:S(2)}) async-start(), calls=%async_computation.19 | async-start | bytes 3981312 | tf_op jit(solution)/shard_map/all_gather | solution.py:207
  18.0 13.1 %copy-start.70 = (bf16[1,96,1536]{2,1,0:T(8,128)(2,1)S(1)}, bf16[1,96,1536]{2,1,0:T(8,128)(2,1)}, u32[]{:S(2)}) copy-start(bf16[1,96,1536]{2,1,0:T(8,128)(2,1)} %param.20) | copy-start | bytes 884740
  18.0 22.1 %copy-start.54 = (bf16[1,192,3072]{2,1,0:T(8,128)(2,1)S(1)}, bf16[1,192,3072]{2,1,0:T(8,128)(2,1)}, u32[]{:S(2)}) copy-start(bf16[1,192,3072]{2,1,0:T(8,128)(2,1)} %param.21) | copy-start | bytes 3538948
  18.0 12.0 %collective-permute-start = (bf16[192,1152]{1,0:T(8,128)(2,1)S(1)}, bf16[192,1152]{1,0:T(8,128)(2,1)S(1)}, u32[]{:S(2)}, u32[]{:S(2)}) collective-permute-start(bf16[192,1152]{1,0:T(8,128)(2,1)S(1)} %broadcast_select_fusion.14), channel_id=1, source_target_pairs={{0,16},{8,24},{16,0},{24,8},{1,17},{9,25},{17,1},{25,9},{2,18},{10... | collective-permute-start | bytes 1327112 | tf_op jit(solution)/shard_map/ppermute | solution.py:114
  31.1 161.0 %all-gather.11.cloned.1.call-start = ((), (), s32[]{:S(2)}) async-start(), calls=%async_computation.20 | async-start | bytes 1327104 | tf_op jit(solution)/shard_map/all_gather | solution.py:164
  31.2 4.8 collective-permute-start.2
  32.3 6.5 collective-permute-start.1
  39.5 179.5 %all-gather.13.cloned.1.call-start = ((), (), s32[]{:S(2)}) async-start(), calls=%async_computation.21 | async-start | bytes 5308416 | tf_op jit(solution)/shard_map/all_gather | solution.py:209
  43.4 15.0 %collective-permute-start.3 = (bf16[192,1536]{1,0:T(8,128)(2,1)S(1)}, bf16[192,1536]{1,0:T(8,128)(2,1)S(1)}, u32[]{:S(2)}, u32[]{:S(2)}) collective-permute-start(bf16[192,1536]{1,0:T(8,128)(2,1)S(1)} %bitcast.256), channel_id=1, source_target_pairs={{0,16},{8,24},{16,0},{24,8},{1,17},{9,25},{17,1},{25,9},{2,18},{10... | collective-permute-start | bytes 1769480 | tf_op jit(solution)/shard_map/ppermute | solution.py:114
  43.5 16.0 %copy-start.53 = (bf16[1,384,1536]{2,1,0:T(8,128)(2,1)S(1)}, bf16[1,384,1536]{2,1,0:T(8,128)(2,1)}, u32[]{:S(2)}) copy-start(bf16[1,384,1536]{2,1,0:T(8,128)(2,1)} %param.22) | copy-start | bytes 3538948
  59.5 168.3 %all-gather.15.cloned.1.call-start = ((), (), s32[]{:S(2)}) async-start(), calls=%async_computation.22 | async-start | bytes 5308416 | tf_op jit(solution)/shard_map/all_gather | solution.py:164
  59.7 6.9 collective-permute-start.5
  59.7 18.6 %copy-start.76 = (f32[2,3,48]{2,0,1:T(2,128)S(1)}, f32[2,3,48]{2,0,1:T(2,128)}, u32[]{:S(2)}) copy-start(f32[2,3,48]{2,0,1:T(2,128)} %param.16) | copy-start | bytes 3460
  59.7 16.3 %collective-permute-start.4 = (bf16[192,1536]{1,0:T(8,128)(2,1)S(1)}, bf16[192,1536]{1,0:T(8,128)(2,1)S(1)}, u32[]{:S(2)}, u32[]{:S(2)}) collective-permute-start(bf16[192,1536]{1,0:T(8,128)(2,1)S(1)} %get-tuple-element.130), channel_id=1, source_target_pairs={{0,0},{1,16},{2,2},{3,18},{4,4},{5,20},{6,6},{7,22},{8,8},{9,24},{... | collective-permute-start | bytes 1769480 | tf_op jit(solution)/shard_map/ppermute | solution.py:152
  77.1 57.7 %copy-start.75 = (s32[1,1024]{1,0:T(1,128)S(1)}, s32[1,1024]{1,0:T(1,128)}, u32[]{:S(2)}) copy-start(s32[1,1024]{1,0:T(1,128)} %param.14) | copy-start | bytes 12292
  77.1 57.7 %copy-start.79 = (s32[1,4]{1,0:T(1,128)S(1)}, s32[1,4]{1,0:T(1,128)}, u32[]{:S(2)}) copy-start(s32[1,4]{1,0:T(1,128)} %param.15) | copy-start | bytes 52
  77.1 177.0 %all-gather.17.cloned.1.call-start = ((), (), s32[]{:S(2)}) async-start(), calls=%async_computation.23 | async-start | bytes 3981312 | tf_op jit(solution)/shard_map/all_gather | solution.py:207
  77.7 214.5 %all-gather.19.cloned.1.call-start = ((), (), s32[]{:S(2)}) async-start(), calls=%async_computation.24 | async-start | bytes 1327104 | tf_op jit(solution)/shard_map/all_gather | solution.py:164
  78.3 252.7 %all-gather.21.cloned.1.call-start = ((), (), s32[]{:S(2)}) async-start(), calls=%async_computation.25 | async-start | bytes 5308416 | tf_op jit(solution)/shard_map/all_gather | solution.py:209
  78.4 59.3 %copy-start.2 = (bf16[1024,1536]{1,0:T(8,128)(2,1)S(1)}, bf16[1024,1536]{1,0:T(8,128)(2,1)}, u32[]{:S(2)}) copy-start(bf16[1024,1536]{1,0:T(8,128)(2,1)} %param.13) | copy-start | bytes 9437188
  139.7 25.8 %copy-start.5 = (bf16[256,1536]{1,0:T(8,128)(2,1)S(1)}, bf16[256,1536]{1,0:T(8,128)(2,1)}, u32[]{:S(2)}) copy-start(bf16[256,1536]{1,0:T(8,128)(2,1)} %param.12) | copy-start | bytes 2359300
  194.9 14.3 %all-to-all-start = ((bf16[4,64,1536]{2,1,0:T(8,128)(2,1)}), bf16[4,64,1536]{2,1,0:T(8,128)(2,1)S(1)}, u32[]{:S(2)}, u32[]{:S(2)}) async-start(bf16[4,64,1536]{2,1,0:T(8,128)(2,1)} %bitcast.218), calls=%async_computation | async-start | bytes 1572864 | tf_op jit(solution)/shard_map/all_to_all | solution.py:184
  198.4 185.3 %all-gather.23.cloned.1.call-start = ((), (), s32[]{:S(2)}) async-start(), calls=%async_computation.26 | async-start | bytes 5308416 | tf_op jit(solution)/shard_map/all_gather | solution.py:164
  219.0 8.8 copy-start.12
  232.8 30.4 %all-to-all-start.1 = ((bf16[4,64,1536]{2,1,0:T(8,128)(2,1)}), bf16[4,64,1536]{2,1,0:T(8,128)(2,1)S(1)}, u32[]{:S(2)}, u32[]{:S(2)}) async-start(bf16[4,64,1536]{2,1,0:T(8,128)(2,1)} %bitcast.252), calls=%async_computation.1 | async-start | bytes 1572864 | tf_op jit(solution)/shard_map/all_to_all | solution.py:184
  263.1 11.7 %copy-start.7 = (bf16[1536,1152]{1,0:T(8,128)(2,1)S(1)}, bf16[1536,1152]{1,0:T(8,128)(2,1)}, u32[]{:S(2)}) copy-start(bf16[1536,1152]{1,0:T(8,128)(2,1)} %all-gather.17.cloned.1.call-done) | copy-start | bytes 10616836
  279.9 6.5 copy-start.9
  295.0 13.8 %all-to-all-start.2 = ((bf16[4,64,1536]{2,1,0:T(8,128)(2,1)}), bf16[4,64,1536]{2,1,0:T(8,128)(2,1)S(1)}, u32[]{:S(2)}, u32[]{:S(2)}) async-start(bf16[4,64,1536]{2,1,0:T(8,128)(2,1)} %bitcast.219), calls=%async_computation.2 | async-start | bytes 1572864 | tf_op jit(solution)/shard_map/all_to_all | solution.py:184
  298.5 247.4 %copy-start.77 = (f32[64]{0:T(128)}, f32[64]{0:T(128)S(1)}, u32[]{:S(2)}) copy-start(f32[64]{0:T(128)S(1)} %add_rsqrt_fusion.2) | copy-start | bytes 772
  383.7 7.8 copy-start.81
  393.9 14.9 %all-to-all-start.5 = ((bf16[4,64,1536]{2,1,0:T(8,128)(2,1)}), bf16[4,64,1536]{2,1,0:T(8,128)(2,1)}, u32[]{:S(2)}, u32[]{:S(2)}) async-start(bf16[4,64,1536]{2,1,0:T(8,128)(2,1)} %bitcast.253), calls=%async_computation.5 | async-start | bytes 1572864 | tf_op jit(solution)/shard_map/all_to_all | solution.py:184
  408.8 14.5 %all-to-all-start.3 = ((bf16[4,64,1536]{2,1,0:T(8,128)(2,1)}), bf16[4,64,1536]{2,1,0:T(8,128)(2,1)}, u32[]{:S(2)}, u32[]{:S(2)}) async-start(bf16[4,64,1536]{2,1,0:T(8,128)(2,1)} %bitcast.250), calls=%async_computation.3 | async-start | bytes 1572864 | tf_op jit(solution)/shard_map/all_to_all | solution.py:184
  424.6 12.0 %copy-start.56 = (bf16[384,1536]{1,0:T(8,128)(2,1)S(1)}, bf16[384,1536]{1,0:T(8,128)(2,1)}, u32[]{:S(2)}) copy-start(bf16[384,1536]{1,0:T(8,128)(2,1)} %all-gather.19.cloned.1.call-done) | copy-start | bytes 3538948
  452.1 13.0 %all-to-all-start.6 = ((bf16[4,64,1536]{2,1,0:T(8,128)(2,1)}), bf16[4,64,1536]{2,1,0:T(8,128)(2,1)}, u32[]{:S(2)}, u32[]{:S(2)}) async-start(bf16[4,64,1536]{2,1,0:T(8,128)(2,1)} %bitcast.33), calls=%async_computation.6 | async-start | bytes 1572864 | tf_op jit(solution)/shard_map/all_to_all | solution.py:184
  456.5 151.7 %reduce-scatter.18.cloned.1.call-start = ((), (), s32[]{:S(2)}) async-start(), calls=%async_computation.29 | async-start | bytes 1327104 | tf_op jit(solution)/shard_map/reduce_scatter | solution.py:177
  465.2 12.4 %copy-start.82 = (f32[256,1536]{1,0:T(8,128)S(1)}, f32[256,1536]{1,0:T(8,128)}, u32[]{:S(2)}) copy-start(f32[256,1536]{1,0:T(8,128)} %get-tuple-element.110) | copy-start | bytes 4718596
  465.2 12.4 %copy-start.83 = (f32[256,1536]{1,0:T(8,128)S(1)}, f32[256,1536]{1,0:T(8,128)}, u32[]{:S(2)}) copy-start(f32[256,1536]{1,0:T(8,128)} %get-tuple-element.163) | copy-start | bytes 4718596
  466.6 15.4 %slice-start.4 = ((s8[4718592]{0:T(1024)(128)(4,1)}), s8[4194304]{0:T(1024)(128)(4,1)S(1)}, s32[]{:S(2)}) async-start(s8[4718592]{0:T(1024)(128)(4,1)} %bitcast.264), calls=%async_computation.41 | async-start | bytes 8388608
  484.4 12.5 %all-to-all-start.7 = ((bf16[4,64,1536]{2,1,0:T(8,128)(2,1)}), bf16[4,64,1536]{2,1,0:T(8,128)(2,1)}, u32[]{:S(2)}, u32[]{:S(2)}) async-start(bf16[4,64,1536]{2,1,0:T(8,128)(2,1)} %bitcast.251), calls=%async_computation.7 | async-start | bytes 1572864 | tf_op jit(solution)/shard_map/all_to_all | solution.py:184
  498.5 10.9 copy-start.55
  499.5 12.3 %copy-start.21 = (bf16[1280,384]{0,1:T(8,128)(2,1)S(1)}, bf16[1280,384]{0,1:T(8,128)(2,1)}, u32[]{:S(2)}) copy-start(bf16[1280,384]{0,1:T(8,128)(2,1)} %copy-done.20) | copy-start | bytes 2949124
  526.2 18.4 %all-to-all-start.8 = ((bf16[4,64,1536]{2,1,0:T(8,128)(2,1)}), bf16[4,64,1536]{2,1,0:T(8,128)(2,1)}, u32[]{:S(2)}, u32[]{:S(2)}) async-start(bf16[4,64,1536]{2,1,0:T(8,128)(2,1)} %bitcast.42), calls=%async_computation.8 | async-start | bytes 1572864 | tf_op jit(solution)/shard_map/all_to_all | solution.py:184
  530.6 77.6 %reduce-scatter.16.cloned.1.call-start = ((), (), s32[]{:S(2)}) async-start(), calls=%async_computation.28 | async-start | bytes 1327104 | tf_op jit(solution)/shard_map/reduce_scatter | solution.py:177
  532.2 138.9 %reduce-scatter.28.cloned.1.call-start = ((), (), s32[]{:S(2)}) async-start(), calls=%async_computation.34 | async-start | bytes 811008
  535.9 10.8 copy-start.74
  553.7 208.3 %all-reduce.2.cloned.1.call-start = ((), (), s32[]{:S(2)}) async-start(), calls=%async_computation.27 | async-start | bytes 6291456 | tf_op jit(solution)/shard_map/psum | solution.py:348
  558.9 247.2 %reduce-scatter.32.cloned.1.call-start = ((), (), s32[]{:S(2)}) async-start(), calls=%async_computation.36 | async-start | bytes 3981312
  570.1 280.6 %reduce-scatter.30.cloned.1.call-start = ((), (), s32[]{:S(2)}) async-start(), calls=%async_computation.35 | async-start | bytes 3981312
  581.3 325.1 %reduce-scatter.22.cloned.1.call-start = ((), (), s32[]{:S(2)}) async-start(), calls=%async_computation.31 | async-start | bytes 5308416 | tf_op jit(solution)/shard_map/reduce_scatter | solution.py:180
  586.2 375.7 %reduce-scatter.20.cloned.1.call-start = ((), (), s32[]{:S(2)}) async-start(), calls=%async_computation.30 | async-start | bytes 5308416 | tf_op jit(solution)/shard_map/reduce_scatter | solution.py:180
  591.2 426.4 %reduce-scatter.26.cloned.1.call-start = ((), (), s32[]{:S(2)}) async-start(), calls=%async_computation.33 | async-start | bytes 5308416 | tf_op jit(solution)/shard_map/reduce_scatter | solution.py:177
  596.3 476.9 %reduce-scatter.24.cloned.1.call-start = ((), (), s32[]{:S(2)}) async-start(), calls=%async_computation.32 | async-start | bytes 5308416 | tf_op jit(solution)/shard_map/reduce_scatter | solution.py:177
  602.8 7.6 all-to-all-start.4
  610.4 62.2 %all-to-all-start.9 = ((bf16[64,4,384]{2,0,1:T(8,128)(2,1)}), bf16[64,4,384]{2,0,1:T(8,128)(2,1)S(1)}, u32[]{:S(2)}, u32[]{:S(2)}) async-start(bf16[64,4,384]{2,0,1:T(8,128)(2,1)} %bitcast.188), calls=%async_computation.9 | async-start | bytes 393216 | tf_op jit(solution)/shard_map/all_to_all | solution.py:191
  613.8 59.6 %collective-permute-start.9 = (bf16[48,1536]{1,0:T(8,128)(2,1)S(1)}, bf16[48,1536]{1,0:T(8,128)(2,1)S(1)}, u32[]{:S(2)}, u32[]{:S(2)}) collective-permute-start(bf16[48,1536]{1,0:T(8,128)(2,1)S(1)} %get-tuple-element.155), channel_id=1, source_target_pairs={{0,0},{16,1},{2,2},{18,3},{4,4},{20,5},{6,6},{22,7},{8,8},{24,9},{... | collective-permute-start | bytes 442376 | tf_op jit(solution)/shard_map/ppermute | solution.py:159
  627.8 45.6 %collective-permute-start.10 = (bf16[48,1536]{1,0:T(8,128)(2,1)S(1)}, bf16[48,1536]{1,0:T(8,128)(2,1)S(1)}, u32[]{:S(2)}, u32[]{:S(2)}) collective-permute-start(bf16[48,1536]{1,0:T(8,128)(2,1)S(1)} %get-tuple-element.156), channel_id=1, source_target_pairs={{1,0},{17,1},{3,2},{19,3},{5,4},{21,5},{7,6},{23,7},{9,8},{25,9},{... | collective-permute-start | bytes 442376 | tf_op jit(solution)/shard_map/ppermute | solution.py:160
  852.2 12.4 %collective-permute-start.8 = (bf16[192,384]{0,1:T(8,128)(2,1)S(1)}, bf16[192,384]{0,1:T(8,128)(2,1)S(1)}, u32[]{:S(2)}, u32[]{:S(2)}) collective-permute-start(bf16[192,384]{0,1:T(8,128)(2,1)S(1)} %broadcast_select_fusion.18), channel_id=1, source_target_pairs={{0,16},{8,24},{16,0},{24,8},{1,17},{9,25},{17,1},{25,9},{2,18},{10... | collective-permute-start | bytes 442376 | tf_op jit(solution)/shard_map/ppermute | solution.py:114
  853.5 6.6 collective-permute-start.7
  853.9 10.5 collective-permute-start.6
  963.9 117.4 %collective-permute-start.11 = (bf16[192,1536]{1,0:T(8,128)(2,1)}, bf16[192,1536]{1,0:T(8,128)(2,1)}, u32[]{:S(2)}, u32[]{:S(2)}) collective-permute-start(bf16[192,1536]{1,0:T(8,128)(2,1)} %broadcast_select_fusion.8), channel_id=1, source_target_pairs={{0,16},{8,24},{16,0},{24,8},{1,17},{9,25},{17,1},{25,9},{2,18},{10... | collective-permute-start | bytes 1769480 | tf_op jit(solution)/shard_map/ppermute | solution.py:114
  970.7 110.6 %copy-start.41 = (bf16[192,1536]{1,0:T(8,128)(2,1)S(1)}, bf16[192,1536]{1,0:T(8,128)(2,1)}, u32[]{:S(2)}) copy-start(bf16[192,1536]{1,0:T(8,128)(2,1)} %reduce-scatter.22.cloned.1.call-done) | copy-start | bytes 1769476
  970.8 110.6 %copy-start.42 = (bf16[192,1536]{1,0:T(8,128)(2,1)S(1)}, bf16[192,1536]{1,0:T(8,128)(2,1)}, u32[]{:S(2)}) copy-start(bf16[192,1536]{1,0:T(8,128)(2,1)} %reduce-scatter.20.cloned.1.call-done) | copy-start | bytes 1769476
  1075.6 18.7 %collective-permute-start.12 = (bf16[192,1536]{1,0:T(8,128)(2,1)}, bf16[192,1536]{1,0:T(8,128)(2,1)S(1)}, u32[]{:S(2)}, u32[]{:S(2)}) collective-permute-start(bf16[192,1536]{1,0:T(8,128)(2,1)} %get-tuple-element.123), channel_id=1, source_target_pairs={{0,0},{16,1},{2,2},{18,3},{4,4},{20,5},{6,6},{22,7},{8,8},{24,9},{... | collective-permute-start | bytes 1769480 | tf_op jit(solution)/shard_map/ppermute | solution.py:159
  1081.3 14.2 %collective-permute-start.13 = (bf16[192,1536]{1,0:T(8,128)(2,1)}, bf16[192,1536]{1,0:T(8,128)(2,1)}, u32[]{:S(2)}, u32[]{:S(2)}) collective-permute-start(bf16[192,1536]{1,0:T(8,128)(2,1)} %get-tuple-element.124), channel_id=1, source_target_pairs={{1,0},{17,1},{3,2},{19,3},{5,4},{21,5},{7,6},{23,7},{9,8},{25,9},{... | collective-permute-start | bytes 1769480 | tf_op jit(solution)/shard_map/ppermute | solution.py:160
  (68 other events, 189.1 us)
Sparse Core Ops, SparseCore 0:
  31.2 43.9 all-gather.8
  77.4 24.9 all-gather.10
  104.6 54.4 all-gather.12
  161.2 51.0 all-gather.14
  213.7 40.3 all-gather.16
  255.6 21.5 all-gather.18
  279.4 51.4 all-gather.20
  333.1 50.5 all-gather.22
  459.6 32.5 reduce-scatter.17
  534.0 36.2 reduce-scatter.15
  575.4 95.6 reduce-scatter.27
  674.0 87.8 all-reduce.1
  764.4 41.6 reduce-scatter.31
  808.3 42.2 reduce-scatter.29
  852.9 53.4 reduce-scatter.21
  908.6 53.3 reduce-scatter.19
  964.2 53.3 reduce-scatter.25
  1019.9 53.3 reduce-scatter.23
where the time goes:
time: 1120 us; the launch traced here: 1110 us
  waiting for transfers between devices  578 us (52%)
  matrix products  153 us (14%)
  blocking collectives  115 us (10%)
  local copies, waits for them, and re-layouts  105 us (9%)
  starting transfers between devices  76.1 us (7%)
  other arithmetic  62.5 us (6%)
  between operations  16.7 us (1%)
    unnamed x21, waiting for transfers between devices  126 us
    reduce_scatter x4, waiting for transfers between devices, scatter_rows(): lax.psum_scatter(grad.astype(low), 'dp', scatter_dimension=0, tiled=True)  101 us
    reduce_scatter x2, waiting for transfers between devices, scatter_columns(): lax.psum_scatter(grad.astype(low), 'dp', scatter_dimension=0, tiled=True)  97.3 us
    psum x1, waiting for transfers between devices, per_device(): lax.psum(norm_back(media_unit, media_inverse, media_scaled).astype(low),...  87.7 us
    all_gather x6, blocking collectives, from_slots(): return lax.all_gather(rows, 'section', axis=0, tiled=True)  58.7 us
    all_gather x1, blocking collectives, per_device(): all_gains = lax.all_gather(gains, ('section', 'dp'), axis=2, tiled=True)  56.3 us
    dot_general x12, matrix products, matmul(): return jnp.dot(left, right, preferred_element_type=full)  53.5 us
    dot_general x16, matrix products, matmul_nt(): lax.dot_general(left, right, (((1,), (1,)), ((), ())), preferred_element_...  50 us
  transfers between devices with their start and end apart: 42, of which 25 were waited for; matrix products, arithmetic and copies ran while one was open for 24% of the time, Pallas kernels for 0%

commit v1 on v0

--- a/solution.py
+++ b/solution.py
@@ -161,7 +161,14 @@
         return jnp.concatenate(pick(near, far), axis=0).astype(full)
 
     def gather_rows(piece):
-        gathered = lax.all_gather(piece, "dp", axis=0, tiled=True)
+        ring = [piece]
+        for hop in range(7):
+            ring.append(lax.ppermute(ring[-1], "dp", [(dev, (dev + 1) % 8) for dev in range(8)]))
+        gathered = jnp.roll(
+            jnp.concatenate(ring[::-1], axis=0),
+            (lax.axis_index("dp") + 1) * ring[0].shape[0],
+            axis=0,
+        )
         if stride > 1:
             width = gathered.shape[1]
             gathered = gathered.reshape(-1, 2, stride, piece.shape[0], width)

time: 1120 us -> 1220 us (1.089)
  starting transfers between devices: 76.1 us -> 136 us
  blocking collectives: 115 us -> 137 us
  local copies, waits for them, and re-layouts: 105 us -> 125 us
  waiting for transfers between devices: 578 us -> 564 us
    ppermute x0 -> x28, waiting for transfers between devices: none -> 99.7 us  [gather_rows(): lax.ppermute(ring[-1], 'dp', [(dev, (dev + 1) % 8) for dev in range(8)])]
    ppermute x0 -> x28, starting transfers between devices: none -> 58 us  [gather_rows(): lax.ppermute(ring[-1], 'dp', [(dev, (dev + 1) % 8) for dev in range(8)])]
    all_gather x4 -> x0, waiting for transfers between devices: 44.4 us -> none  [gather_rows(): gathered = lax.all_gather(piece, 'dp', axis=0, tiled=True)]
    unnamed x199 -> x313, local copies, waits for them, and re-layouts: 32.9 us -> 55.8 us
    all_to_all x8, waiting for transfers between devices: 35.1 us -> 13.7 us  [sum_to_slots(): arrived = lax.all_to_all(blocks, 'section', split_axis=0, concat_axis=0)]
    all_gather x2, waiting for transfers between devices: 17.8 us -> 0.02 us  [per_device(): qkv_w.append(lax.all_gather(qkv_pieces[layer], 'dp', axis=0, tiled=True))]
    all_gather x6, blocking collectives: 58.7 us -> 75.5 us  [from_slots(): return lax.all_gather(rows, 'section', axis=0, tiled=True)]
    ppermute x2, waiting for transfers between devices: 12.3 us -> 0.01 us  [exchange_rows(): first = lax.ppermute(near, ('section', 'dp'), turn_pairs(0, False))]
  transfers between devices with their start and end apart: 42 -> 66, of which waited for: 25 -> 35; matrix products, arithmetic and copies ran while one was open for 24% -> 24% of each run, Pallas kernels for 0% -> 0%
where the time goes in v1:
time: 1220 us; the launch traced here: 1210 us
  waiting for transfers between devices  564 us (46%)
  matrix products  155 us (13%)
  blocking collectives  137 us (11%)
  starting transfers between devices  136 us (11%)
  local copies, waits for them, and re-layouts  125 us (10%)
  other arithmetic  73.5 us (6%)
  between operations  17 us (1%)
    unnamed x17, waiting for transfers between devices  124 us
    reduce_scatter x4, waiting for transfers between devices, scatter_rows(): lax.psum_scatter(grad.astype(low), 'dp', scatter_dimension=0, tiled=True)  101 us
    ppermute x28, waiting for transfers between devices, gather_rows(): lax.ppermute(ring[-1], 'dp', [(dev, (dev + 1) % 8) for dev in range(8)])  99.7 us
    reduce_scatter x2, waiting for transfers between devices, scatter_columns(): lax.psum_scatter(grad.astype(low), 'dp', scatter_dimension=0, tiled=True)  97.5 us
    psum x1, waiting for transfers between devices, per_device(): lax.psum(norm_back(media_unit, media_inverse, media_scaled).astype(low),...  87.8 us
    all_gather x6, blocking collectives, from_slots(): return lax.all_gather(rows, 'section', axis=0, tiled=True)  75.5 us
    all_gather x1, blocking collectives, per_device(): all_gains = lax.all_gather(gains, ('section', 'dp'), axis=2, tiled=True)  61.2 us
    ppermute x28, starting transfers between devices, gather_rows(): lax.ppermute(ring[-1], 'dp', [(dev, (dev + 1) % 8) for dev in range(8)])  58 us
  transfers between devices with their start and end apart: 66, of which 35 were waited for; matrix products, arithmetic and copies ran while one was open for 24% of the time, Pallas kernels for 0%

profile of v1, /device:TPU:1, one launch (start us, length us, event | category | flops | bytes accessed | tf_op | source)
XLA Modules:
  0.0 1207.9 jit_solution(11632075617216092441)
XLA Ops:
  20.1 9.9 collective-permute-done
  35.9 12.5 %collective-permute-done.10 = bf16[192,1536]{1,0:T(8,128)(2,1)S(1)} collective-permute-done((bf16[192,1536]{1,0:T(8,128)(2,1)S(1)}, bf16[192,1536]{1,0:T(8,128)(2,1)S(1)}, u32[]{:S(2)}, u32[]{:S(2)}) %collective-permute-start.10) | collective-permute-done | bytes 589856 | tf_op jit(solution)/shard_map/ppermute | solution.py:114
  51.1 4.8 collective-permute-start.1
  60.5 61.2 %all_gather.33 = f32[2,3,1536]{1,0,2:T(2,128)S(1)} all-gather(f32[2,3,48]{1,0,2:T(2,128)S(1)} %copy.170), channel_id=1, replica_groups=mesh['section'=4,'dp'=8] {'section','dp'}, dimensions={2}, use_global_device_ids=true | all-gather | bytes 38016 | tf_op jit(solution)/shard_map/all_gather | solution.py:221
  123.4 26.1 %slice_reduce_fusion = (f32[1536]{0:T(1024)}, f32[1536]{0:T(1024)S(1)}, f32[1536]{0:T(1024)S(1)}, f32[1536]{0:T(1024)S(1)}, f32[1536]{0:T(1024)S(1)}, /*index=5*/f32[1536]{0:T(1024)S(1)}) fusion(f32[2,3,1536]{1,0,2:T(2,128)S(1)} %all_gather.33), kind=kLoop, calls=%fused_computation.178 | loop fusion | bytes 73728 | tf_op jit(solution)/shard_map/slice | solution.py:266
  155.2 4.8 collective-permute-done.3
  181.5 8.6 collective-permute-done.22
  197.2 9.3 collective-permute-start.8
  212.0 4.9 collective-permute-done.25
  224.8 8.6 collective-permute-done.28
  235.8 16.6 %collective-permute-done.15 = bf16[192,1536]{1,0:T(8,128)(2,1)S(1)} collective-permute-done((bf16[192,1536]{1,0:T(8,128)(2,1)}, bf16[192,1536]{1,0:T(8,128)(2,1)S(1)}, u32[]{:S(2)}, u32[]{:S(2)}) %collective-permute-start.15) | collective-permute-done | bytes 589856 | tf_op jit(solution)/shard_map/ppermute | solution.py:166
  255.8 15.5 %collective-permute-done.29 = bf16[192,1536]{1,0:T(8,128)(2,1)S(1)} collective-permute-done((bf16[192,1536]{1,0:T(8,128)(2,1)S(1)}, bf16[192,1536]{1,0:T(8,128)(2,1)S(1)}, u32[]{:S(2)}, u32[]{:S(2)}) %collective-permute-start.29) | collective-permute-done | bytes 589856 | tf_op jit(solution)/shard_map/ppermute | solution.py:166
  273.7 12.1 collective-permute-done.16
  294.6 3.8 collective-permute-done.17
  307.2 3.8 collective-permute-done.18
  313.6 3.8 collective-permute-done.32
  319.9 3.8 collective-permute-done.19
  343.2 4.1 convolution_convert_fusion.24
  348.0 4.0 convolution_convert_fusion.25
  365.3 9.2 fusion.18
  375.2 11.7 all_gather.35
  386.9 8.3 multiply_convert_fusion.3
  395.2 4.9 convolution_convert_fusion.21
  403.7 5.1 convolution_convert_fusion.22
  408.7 3.9 convolution_convert_fusion.23
  413.3 12.0 all_gather.38
  448.1 4.7 all-to-all-done.2
  453.4 13.2 %all_gather.39 = bf16[256,1536]{1,0:T(8,128)(2,1)} all-gather(bf16[64,1536]{1,0:T(8,128)(2,1)S(1)} %multiply_convert_fusion.4), channel_id=1, replica_groups=mesh['section'=4,'dp'=8] {'section'}, dimensions={0}, use_global_device_ids=true | all-gather | bytes 983040 | tf_op jit(solution)/shard_map/all_gather | solution.py:195
  466.6 8.1 multiply_convert_fusion.2
  474.7 9.3 add_convert_fusion.1
  486.3 4.4 all-to-all-start.5
  490.7 7.4 convolution_convert_fusion.20
  498.1 4.2 all-to-all-start.3
  503.8 9.0 all-to-all-done.3
  516.1 12.5 %all_gather.41 = bf16[256,1536]{1,0:T(8,128)(2,1)S(1)} all-gather(bf16[64,1536]{1,0:T(8,128)(2,1)S(1)} %get-tuple-element.105), channel_id=1, replica_groups=mesh['section'=4,'dp'=8] {'section'}, dimensions={0}, use_global_device_ids=true | all-gather | bytes 983040 | tf_op jit(solution)/shard_map/all_gather | solution.py:195
  545.6 4.3 all-to-all-start.6
  553.0 5.8 fusion.64
  561.5 13.2 %all_gather.42 = bf16[256,1536]{1,0:T(8,128)(2,1)S(1)} all-gather(bf16[64,1536]{1,0:T(8,128)(2,1)S(1)} %get-tuple-element.103), channel_id=1, replica_groups=mesh['section'=4,'dp'=8] {'section'}, dimensions={0}, use_global_device_ids=true | all-gather | bytes 983040 | tf_op jit(solution)/shard_map/all_gather | solution.py:195
  574.6 5.3 add_convert_fusion
  582.3 4.3 all-to-all-start.7
  586.7 7.7 convolution_add_fusion.1
  597.0 13.0 %all_gather.43 = bf16[256,1536]{1,0:T(8,128)(2,1)S(1)} all-gather(bf16[64,1536]{1,0:T(8,128)(2,1)S(1)} %get-tuple-element.101), channel_id=1, replica_groups=mesh['section'=4,'dp'=8] {'section'}, dimensions={0}, use_global_device_ids=true | all-gather | bytes 983040 | tf_op jit(solution)/shard_map/all_gather | solution.py:195
  611.5 3.9 multiply_reduce_fusion
  626.0 4.3 all-to-all-start.8
  635.8 8.6 fusion.101
  653.1 5.1 fusion.13
  659.8 3.7 convolution_convert_fusion.4
  665.6 3.8 copy.202
  671.0 3.8 convolution_convert_fusion.6
  676.8 3.8 copy.200
  713.1 17.0 %collective-permute-start.37 = (bf16[48,1536]{1,0:T(8,128)(2,1)S(1)}, bf16[48,1536]{1,0:T(8,128)(2,1)S(1)}, u32[]{:S(2)}, u32[]{:S(2)}) collective-permute-start(bf16[48,1536]{1,0:T(8,128)(2,1)S(1)} %get-tuple-element.157), channel_id=1, source_target_pairs={{0,0},{16,1},{2,2},{18,3},{4,4},{20,5},{6,6},{22,7},{8,8},{24,9},{... | collective-permute-start | bytes 442376 | tf_op jit(solution)/shard_map/ppermute | solution.py:159
  730.9 42.3 %reduce-scatter.28.cloned.1.call-done = f32[48,6]{1,0:T(8,128)} async-done(((f32[1536,6]{1,0:T(8,128)}), f32[48,6]{1,0:T(8,128)}) %reduce-scatter.28.cloned.1.call-update) | async-done | bytes 1168
  776.4 87.8 %all-reduce.2.cloned.1.call-done = bf16[1024,1536]{1,0:T(8,128)(2,1)} async-done(((bf16[1024,1536]{1,0:T(8,128)(2,1)}), bf16[1024,1536]{1,0:T(8,128)(2,1)}) %all-reduce.2.cloned.1.call-update) | async-done | bytes 3145744 | tf_op jit(solution)/shard_map/psum | solution.py:355
  864.3 5.5 convert_element_type.431
  869.7 38.7 %reduce-scatter.32.cloned.1.call-done = bf16[192,1152]{1,0:T(8,128)(2,1)} async-done(((bf16[1536,1152]{1,0:T(8,128)(2,1)}), bf16[192,1152]{1,0:T(8,128)(2,1)}) %reduce-scatter.32.cloned.1.call-update) | async-done | bytes 442384
  910.0 43.0 %reduce-scatter.30.cloned.1.call-done = bf16[192,1152]{1,0:T(8,128)(2,1)} async-done(((bf16[1536,1152]{1,0:T(8,128)(2,1)}), bf16[192,1152]{1,0:T(8,128)(2,1)}) %reduce-scatter.30.cloned.1.call-update) | async-done | bytes 442384
  957.4 4.9 collective-permute-done.35
  962.4 4.3 collective-permute-done.34
  967.0 41.8 %reduce-scatter.22.cloned.1.call-done = bf16[192,1536]{1,0:T(8,128)(2,1)} async-done(((bf16[1536,1536]{1,0:T(8,128)(2,1)}), bf16[192,1536]{1,0:T(8,128)(2,1)}) %reduce-scatter.22.cloned.1.call-update) | async-done | bytes 589840 | tf_op jit(solution)/shard_map/reduce_scatter | solution.py:187
  1008.8 55.6 %reduce-scatter.20.cloned.1.call-done = bf16[192,1536]{1,0:T(8,128)(2,1)} async-done(((bf16[1536,1536]{1,0:T(8,128)(2,1)}), bf16[192,1536]{1,0:T(8,128)(2,1)}) %reduce-scatter.20.cloned.1.call-update) | async-done | bytes 589840 | tf_op jit(solution)/shard_map/reduce_scatter | solution.py:187
  1075.0 45.2 %reduce-scatter.26.cloned.1.call-done = bf16[192,1536]{1,0:T(8,128)(2,1)} async-done(((bf16[1536,1536]{1,0:T(8,128)(2,1)}), bf16[192,1536]{1,0:T(8,128)(2,1)}) %reduce-scatter.26.cloned.1.call-update) | async-done | bytes 589840 | tf_op jit(solution)/shard_map/reduce_scatter | solution.py:184
  1120.2 55.6 %reduce-scatter.24.cloned.1.call-done = bf16[192,1536]{1,0:T(8,128)(2,1)} async-done(((bf16[1536,1536]{1,0:T(8,128)(2,1)}), bf16[192,1536]{1,0:T(8,128)(2,1)}) %reduce-scatter.24.cloned.1.call-update) | async-done | bytes 589840 | tf_op jit(solution)/shard_map/reduce_scatter | solution.py:184
  1178.1 5.8 collective-permute-start.40
  1190.5 6.3 collective-permute-done.40
  (623 shorter events, 300.7 us)
Async XLA Ops:
  7.2 332.6 %all-gather.5.cloned.1.call-start = ((), (), s32[]{:S(2)}) async-start(), calls=%async_computation.19 | async-start | bytes 3981312 | tf_op jit(solution)/shard_map/all_gather | solution.py:214
  18.0 12.0 collective-permute-start
  31.1 355.8 %all-gather.7.cloned.1.call-start = ((), (), s32[]{:S(2)}) async-start(), calls=%async_computation.20 | async-start | bytes 5308416 | tf_op jit(solution)/shard_map/all_gather | solution.py:216
  34.6 13.8 %collective-permute-start.10 = (bf16[192,1536]{1,0:T(8,128)(2,1)S(1)}, bf16[192,1536]{1,0:T(8,128)(2,1)S(1)}, u32[]{:S(2)}, u32[]{:S(2)}) collective-permute-start(bf16[192,1536]{1,0:T(8,128)(2,1)S(1)} %bitcast.246), channel_id=1, source_target_pairs={{0,16},{8,24},{16,0},{24,8},{1,17},{9,25},{17,1},{25,9},{2,18},{10... | collective-permute-start | bytes 1769480 | tf_op jit(solution)/shard_map/ppermute | solution.py:114
  49.5 354.1 %all-gather.9.cloned.1.call-start = ((), (), s32[]{:S(2)}) async-start(), calls=%async_computation.21 | async-start | bytes 3981312 | tf_op jit(solution)/shard_map/all_gather | solution.py:214
  50.3 102.8 %collective-permute-start.2 = (bf16[48,1536]{1,0:T(8,128)(2,1)}, bf16[48,1536]{1,0:T(8,128)(2,1)S(1)}, u32[]{:S(2)}, u32[]{:S(2)}) collective-permute-start(bf16[48,1536]{1,0:T(8,128)(2,1)} %get-tuple-element.161), channel_id=1, source_target_pairs={{0,1},{1,17},{2,3},{3,19},{4,5},{5,21},{6,7},{7,23},{8,9},{9,25},{... | collective-permute-start | bytes 442376 | tf_op jit(solution)/shard_map/ppermute | solution.py:153
  51.1 102.6 %collective-permute-start.1 = (bf16[48,1536]{1,0:T(8,128)(2,1)S(1)}, bf16[48,1536]{1,0:T(8,128)(2,1)}, u32[]{:S(2)}, u32[]{:S(2)}) collective-permute-start(bf16[48,1536]{1,0:T(8,128)(2,1)S(1)} %get-tuple-element.162), channel_id=1, source_target_pairs={{0,0},{1,16},{2,2},{3,18},{4,4},{5,20},{6,6},{7,22},{8,8},{9,24},{... | collective-permute-start | bytes 442376 | tf_op jit(solution)/shard_map/ppermute | solution.py:152
  55.9 410.7 %all-gather.11.cloned.1.call-start = ((), (), s32[]{:S(2)}) async-start(), calls=%async_computation.22 | async-start | bytes 5308416 | tf_op jit(solution)/shard_map/all_gather | solution.py:216
  58.4 113.6 %collective-permute-start.12 = (bf16[192,1536]{1,0:T(8,128)(2,1)}, bf16[192,1536]{1,0:T(8,128)(2,1)}, u32[]{:S(2)}, u32[]{:S(2)}) collective-permute-start(bf16[192,1536]{1,0:T(8,128)(2,1)} %get-tuple-element.131), channel_id=1, source_target_pairs={{0,1},{1,17},{2,3},{3,19},{4,5},{5,21},{6,7},{7,23},{8,9},{9,25},{... | collective-permute-start | bytes 1769480 | tf_op jit(solution)/shard_map/ppermute | solution.py:153
  58.4 113.6 %collective-permute-start.11 = (bf16[192,1536]{1,0:T(8,128)(2,1)}, bf16[192,1536]{1,0:T(8,128)(2,1)}, u32[]{:S(2)}, u32[]{:S(2)}) collective-permute-start(bf16[192,1536]{1,0:T(8,128)(2,1)} %get-tuple-element.132), channel_id=1, source_target_pairs={{0,0},{1,16},{2,2},{3,18},{4,4},{5,20},{6,6},{7,22},{8,8},{9,24},{... | collective-permute-start | bytes 1769480 | tf_op jit(solution)/shard_map/ppermute | solution.py:152
  155.1 9.6 collective-permute-start.20
  160.0 9.5 collective-permute-start.4
  164.8 11.4 collective-permute-start.21
  169.5 9.5 collective-permute-start.5
  173.3 33.2 %collective-permute-start.13 = (bf16[192,1536]{1,0:T(8,128)(2,1)S(1)}, bf16[192,1536]{1,0:T(8,128)(2,1)}, u32[]{:S(2)}, u32[]{:S(2)}) collective-permute-start(bf16[192,1536]{1,0:T(8,128)(2,1)S(1)} %get-tuple-element.128), channel_id=1, source_target_pairs={{0,1},{1,2},{2,3},{3,4},{4,5},{5,6},{6,7},{7,0},{8,9},{9,10},{10,1... | collective-permute-start | bytes 1769480 | tf_op jit(solution)/shard_map/ppermute | solution.py:166
  176.1 13.9 %collective-permute-start.22 = (bf16[48,1536]{1,0:T(8,128)(2,1)S(1)}, bf16[48,1536]{1,0:T(8,128)(2,1)S(1)}, u32[]{:S(2)}, u32[]{:S(2)}) collective-permute-start(bf16[48,1536]{1,0:T(8,128)(2,1)S(1)} %collective-permute-done.21), channel_id=1, source_target_pairs={{0,1},{1,2},{2,3},{3,4},{4,5},{5,6},{6,7},{7,0},{8,9},{9,10},{10,1... | collective-permute-start | bytes 442376 | tf_op jit(solution)/shard_map/ppermute | solution.py:166
  179.0 13.6 %collective-permute-start.6 = (bf16[48,1536]{1,0:T(8,128)(2,1)S(1)}, bf16[48,1536]{1,0:T(8,128)(2,1)S(1)}, u32[]{:S(2)}, u32[]{:S(2)}) collective-permute-start(bf16[48,1536]{1,0:T(8,128)(2,1)S(1)} %collective-permute-done.5), channel_id=1, source_target_pairs={{0,1},{1,2},{2,3},{3,4},{4,5},{5,6},{6,7},{7,0},{8,9},{9,10},{10,1... | collective-permute-start | bytes 442376 | tf_op jit(solution)/shard_map/ppermute | solution.py:166
  190.1 5.3 collective-permute-start.23
  194.2 26.1 %collective-permute-start.27 = (bf16[192,1536]{1,0:T(8,128)(2,1)S(1)}, bf16[192,1536]{1,0:T(8,128)(2,1)}, u32[]{:S(2)}, u32[]{:S(2)}) collective-permute-start(bf16[192,1536]{1,0:T(8,128)(2,1)S(1)} %get-tuple-element.127), channel_id=1, source_target_pairs={{0,1},{1,2},{2,3},{3,4},{4,5},{5,6},{6,7},{7,0},{8,9},{9,10},{10,1... | collective-permute-start | bytes 1769480 | tf_op jit(solution)/shard_map/ppermute | solution.py:166
  195.4 11.7 collective-permute-start.24
  197.2 14.1 %collective-permute-start.8 = (bf16[48,1536]{1,0:T(8,128)(2,1)}, bf16[48,1536]{1,0:T(8,128)(2,1)}, u32[]{:S(2)}, u32[]{:S(2)}) collective-permute-start(bf16[48,1536]{1,0:T(8,128)(2,1)} %collective-permute-done.7), channel_id=1, source_target_pairs={{0,1},{1,2},{2,3},{3,4},{4,5},{5,6},{6,7},{7,0},{8,9},{9,10},{10,1... | collective-permute-start | bytes 442376 | tf_op jit(solution)/shard_map/ppermute | solution.py:166
  206.5 15.4 %collective-permute-start.14 = (bf16[192,1536]{1,0:T(8,128)(2,1)}, bf16[192,1536]{1,0:T(8,128)(2,1)}, u32[]{:S(2)}, u32[]{:S(2)}) collective-permute-start(bf16[192,1536]{1,0:T(8,128)(2,1)} %collective-permute-done.13), channel_id=1, source_target_pairs={{0,1},{1,2},{2,3},{3,4},{4,5},{5,6},{6,7},{7,0},{8,9},{9,10},{10,1... | collective-permute-start | bytes 1769480 | tf_op jit(solution)/shard_map/ppermute | solution.py:166
  207.1 9.7 collective-permute-start.25
  211.4 7.9 collective-permute-start.9
  216.8 71.5 %collective-permute-start.26 = (bf16[48,1536]{1,0:T(8,128)(2,1)}, bf16[48,1536]{1,0:T(8,128)(2,1)S(1)}, u32[]{:S(2)}, u32[]{:S(2)}) collective-permute-start(bf16[48,1536]{1,0:T(8,128)(2,1)} %collective-permute-done.25), channel_id=1, source_target_pairs={{0,1},{1,2},{2,3},{3,4},{4,5},{5,6},{6,7},{7,0},{8,9},{9,10},{10,1... | collective-permute-start | bytes 442376 | tf_op jit(solution)/shard_map/ppermute | solution.py:166
  220.3 13.2 %collective-permute-start.28 = (bf16[192,1536]{1,0:T(8,128)(2,1)}, bf16[192,1536]{1,0:T(8,128)(2,1)S(1)}, u32[]{:S(2)}, u32[]{:S(2)}) collective-permute-start(bf16[192,1536]{1,0:T(8,128)(2,1)} %collective-permute-done.27), channel_id=1, source_target_pairs={{0,1},{1,2},{2,3},{3,4},{4,5},{5,6},{6,7},{7,0},{8,9},{9,10},{10,1... | collective-permute-start | bytes 1769480 | tf_op jit(solution)/shard_map/ppermute | solution.py:166
  221.9 30.5 %collective-permute-start.15 = (bf16[192,1536]{1,0:T(8,128)(2,1)}, bf16[192,1536]{1,0:T(8,128)(2,1)S(1)}, u32[]{:S(2)}, u32[]{:S(2)}) collective-permute-start(bf16[192,1536]{1,0:T(8,128)(2,1)} %collective-permute-done.14), channel_id=1, source_target_pairs={{0,1},{1,2},{2,3},{3,4},{4,5},{5,6},{6,7},{7,0},{8,9},{9,10},{10,1... | collective-permute-start | bytes 1769480 | tf_op jit(solution)/shard_map/ppermute | solution.py:166
  233.4 37.8 %collective-permute-start.29 = (bf16[192,1536]{1,0:T(8,128)(2,1)S(1)}, bf16[192,1536]{1,0:T(8,128)(2,1)S(1)}, u32[]{:S(2)}, u32[]{:S(2)}) collective-permute-start(bf16[192,1536]{1,0:T(8,128)(2,1)S(1)} %collective-permute-done.28), channel_id=1, source_target_pairs={{0,1},{1,2},{2,3},{3,4},{4,5},{5,6},{6,7},{7,0},{8,9},{9,10},{10,1... | collective-permute-start | bytes 1769480 | tf_op jit(solution)/shard_map/ppermute | solution.py:166
  252.4 33.4 %collective-permute-start.16 = (bf16[192,1536]{1,0:T(8,128)(2,1)S(1)}, bf16[192,1536]{1,0:T(8,128)(2,1)S(1)}, u32[]{:S(2)}, u32[]{:S(2)}) collective-permute-start(bf16[192,1536]{1,0:T(8,128)(2,1)S(1)} %collective-permute-done.15), channel_id=1, source_target_pairs={{0,1},{1,2},{2,3},{3,4},{4,5},{5,6},{6,7},{7,0},{8,9},{9,10},{10,1... | collective-permute-start | bytes 1769480 | tf_op jit(solution)/shard_map/ppermute | solution.py:166
  271.2 20.9 %collective-permute-start.30 = (bf16[192,1536]{1,0:T(8,128)(2,1)S(1)}, bf16[192,1536]{1,0:T(8,128)(2,1)S(1)}, u32[]{:S(2)}, u32[]{:S(2)}) collective-permute-start(bf16[192,1536]{1,0:T(8,128)(2,1)S(1)} %collective-permute-done.29), channel_id=1, source_target_pairs={{0,1},{1,2},{2,3},{3,4},{4,5},{5,6},{6,7},{7,0},{8,9},{9,10},{10,1... | collective-permute-start | bytes 1769480 | tf_op jit(solution)/shard_map/ppermute | solution.py:166
  285.8 12.6 %collective-permute-start.17 = (bf16[192,1536]{1,0:T(8,128)(2,1)S(1)}, bf16[192,1536]{1,0:T(8,128)(2,1)S(1)}, u32[]{:S(2)}, u32[]{:S(2)}) collective-permute-start(bf16[192,1536]{1,0:T(8,128)(2,1)S(1)} %collective-permute-done.16), channel_id=1, source_target_pairs={{0,1},{1,2},{2,3},{3,4},{4,5},{5,6},{6,7},{7,0},{8,9},{9,10},{10,1... | collective-permute-start | bytes 1769480 | tf_op jit(solution)/shard_map/ppermute | solution.py:166
  292.1 12.6 %collective-permute-start.31 = (bf16[192,1536]{1,0:T(8,128)(2,1)S(1)}, bf16[192,1536]{1,0:T(8,128)(2,1)S(1)}, u32[]{:S(2)}, u32[]{:S(2)}) collective-permute-start(bf16[192,1536]{1,0:T(8,128)(2,1)S(1)} %collective-permute-done.30), channel_id=1, source_target_pairs={{0,1},{1,2},{2,3},{3,4},{4,5},{5,6},{6,7},{7,0},{8,9},{9,10},{10,1... | collective-permute-start | bytes 1769480 | tf_op jit(solution)/shard_map/ppermute | solution.py:166
  298.4 12.6 %collective-permute-start.18 = (bf16[192,1536]{1,0:T(8,128)(2,1)S(1)}, bf16[192,1536]{1,0:T(8,128)(2,1)S(1)}, u32[]{:S(2)}, u32[]{:S(2)}) collective-permute-start(bf16[192,1536]{1,0:T(8,128)(2,1)S(1)} %collective-permute-done.17), channel_id=1, source_target_pairs={{0,1},{1,2},{2,3},{3,4},{4,5},{5,6},{6,7},{7,0},{8,9},{9,10},{10,1... | collective-permute-start | bytes 1769480 | tf_op jit(solution)/shard_map/ppermute | solution.py:166
  304.8 12.6 %collective-permute-start.32 = (bf16[192,1536]{1,0:T(8,128)(2,1)S(1)}, bf16[192,1536]{1,0:T(8,128)(2,1)S(1)}, u32[]{:S(2)}, u32[]{:S(2)}) collective-permute-start(bf16[192,1536]{1,0:T(8,128)(2,1)S(1)} %collective-permute-done.31), channel_id=1, source_target_pairs={{0,1},{1,2},{2,3},{3,4},{4,5},{5,6},{6,7},{7,0},{8,9},{9,10},{10,1... | collective-permute-start | bytes 1769480 | tf_op jit(solution)/shard_map/ppermute | solution.py:166
  311.1 12.6 %collective-permute-start.19 = (bf16[192,1536]{1,0:T(8,128)(2,1)S(1)}, bf16[192,1536]{1,0:T(8,128)(2,1)S(1)}, u32[]{:S(2)}, u32[]{:S(2)}) collective-permute-start(bf16[192,1536]{1,0:T(8,128)(2,1)S(1)} %collective-permute-done.18), channel_id=1, source_target_pairs={{0,1},{1,2},{2,3},{3,4},{4,5},{5,6},{6,7},{7,0},{8,9},{9,10},{10,1... | collective-permute-start | bytes 1769480 | tf_op jit(solution)/shard_map/ppermute | solution.py:166
  317.4 15.3 %collective-permute-start.33 = (bf16[192,1536]{1,0:T(8,128)(2,1)S(1)}, bf16[192,1536]{1,0:T(8,128)(2,1)S(1)}, u32[]{:S(2)}, u32[]{:S(2)}) collective-permute-start(bf16[192,1536]{1,0:T(8,128)(2,1)S(1)} %collective-permute-done.32), channel_id=1, source_target_pairs={{0,1},{1,2},{2,3},{3,4},{4,5},{5,6},{6,7},{7,0},{8,9},{9,10},{10,1... | collective-permute-start | bytes 1769480 | tf_op jit(solution)/shard_map/ppermute | solution.py:166
  361.6 12.9 %all-to-all-start = ((bf16[4,64,1536]{2,1,0:T(8,128)(2,1)}), bf16[4,64,1536]{2,1,0:T(8,128)(2,1)S(1)}, u32[]{:S(2)}, u32[]{:S(2)}) async-start(bf16[4,64,1536]{2,1,0:T(8,128)(2,1)} %bitcast.243), calls=%async_computation | async-start | bytes 1572864 | tf_op jit(solution)/shard_map/all_to_all | solution.py:191
  400.1 12.6 %all-to-all-start.1 = ((bf16[4,64,1536]{2,1,0:T(8,128)(2,1)}), bf16[4,64,1536]{2,1,0:T(8,128)(2,1)S(1)}, u32[]{:S(2)}, u32[]{:S(2)}) async-start(bf16[4,64,1536]{2,1,0:T(8,128)(2,1)} %bitcast.242), calls=%async_computation.1 | async-start | bytes 1572864 | tf_op jit(solution)/shard_map/all_to_all | solution.py:191
  442.3 10.5 all-to-all-start.2
  486.3 11.8 all-to-all-start.5
  498.1 14.7 %all-to-all-start.3 = ((bf16[4,64,1536]{2,1,0:T(8,128)(2,1)}), bf16[4,64,1536]{2,1,0:T(8,128)(2,1)}, u32[]{:S(2)}, u32[]{:S(2)}) async-start(bf16[4,64,1536]{2,1,0:T(8,128)(2,1)} %bitcast.238), calls=%async_computation.3 | async-start | bytes 1572864 | tf_op jit(solution)/shard_map/all_to_all | solution.py:191
  545.6 13.2 %all-to-all-start.6 = ((bf16[4,64,1536]{2,1,0:T(8,128)(2,1)}), bf16[4,64,1536]{2,1,0:T(8,128)(2,1)}, u32[]{:S(2)}, u32[]{:S(2)}) async-start(bf16[4,64,1536]{2,1,0:T(8,128)(2,1)} %bitcast.33), calls=%async_computation.6 | async-start | bytes 1572864 | tf_op jit(solution)/shard_map/all_to_all | solution.py:191
  550.0 157.6 %reduce-scatter.18.cloned.1.call-start = ((), (), s32[]{:S(2)}) async-start(), calls=%async_computation.25 | async-start | bytes 1327104 | tf_op jit(solution)/shard_map/reduce_scatter | solution.py:184
  582.3 12.1 %all-to-all-start.7 = ((bf16[4,64,1536]{2,1,0:T(8,128)(2,1)}), bf16[4,64,1536]{2,1,0:T(8,128)(2,1)}, u32[]{:S(2)}, u32[]{:S(2)}) async-start(bf16[4,64,1536]{2,1,0:T(8,128)(2,1)} %bitcast.241), calls=%async_computation.7 | async-start | bytes 1572864 | tf_op jit(solution)/shard_map/all_to_all | solution.py:191
  626.0 18.5 %all-to-all-start.8 = ((bf16[4,64,1536]{2,1,0:T(8,128)(2,1)}), bf16[4,64,1536]{2,1,0:T(8,128)(2,1)}, u32[]{:S(2)}, u32[]{:S(2)}) async-start(bf16[4,64,1536]{2,1,0:T(8,128)(2,1)} %bitcast.42), calls=%async_computation.8 | async-start | bytes 1572864 | tf_op jit(solution)/shard_map/all_to_all | solution.py:191
  630.3 77.2 %reduce-scatter.16.cloned.1.call-start = ((), (), s32[]{:S(2)}) async-start(), calls=%async_computation.24 | async-start | bytes 1327104 | tf_op jit(solution)/shard_map/reduce_scatter | solution.py:184
  631.9 141.3 %reduce-scatter.28.cloned.1.call-start = ((), (), s32[]{:S(2)}) async-start(), calls=%async_computation.30 | async-start | bytes 811008
  653.0 211.3 %all-reduce.2.cloned.1.call-start = ((), (), s32[]{:S(2)}) async-start(), calls=%async_computation.23 | async-start | bytes 6291456 | tf_op jit(solution)/shard_map/psum | solution.py:355
  658.2 250.2 %reduce-scatter.32.cloned.1.call-start = ((), (), s32[]{:S(2)}) async-start(), calls=%async_computation.32 | async-start | bytes 3981312
  669.4 283.5 %reduce-scatter.30.cloned.1.call-start = ((), (), s32[]{:S(2)}) async-start(), calls=%async_computation.31 | async-start | bytes 3981312
  680.6 328.2 %reduce-scatter.22.cloned.1.call-start = ((), (), s32[]{:S(2)}) async-start(), calls=%async_computation.27 | async-start | bytes 5308416 | tf_op jit(solution)/shard_map/reduce_scatter | solution.py:187
  685.6 378.8 %reduce-scatter.20.cloned.1.call-start = ((), (), s32[]{:S(2)}) async-start(), calls=%async_computation.26 | async-start | bytes 5308416 | tf_op jit(solution)/shard_map/reduce_scatter | solution.py:187
  690.6 429.6 %reduce-scatter.26.cloned.1.call-start = ((), (), s32[]{:S(2)}) async-start(), calls=%async_computation.29 | async-start | bytes 5308416 | tf_op jit(solution)/shard_map/reduce_scatter | solution.py:184
  695.6 480.2 %reduce-scatter.24.cloned.1.call-start = ((), (), s32[]{:S(2)}) async-start(), calls=%async_computation.28 | async-start | bytes 5308416 | tf_op jit(solution)/shard_map/reduce_scatter | solution.py:184
  702.1 7.6 all-to-all-start.4
  709.7 65.0 %all-to-all-start.9 = ((bf16[64,4,384]{2,0,1:T(8,128)(2,1)}), bf16[64,4,384]{2,0,1:T(8,128)(2,1)S(1)}, u32[]{:S(2)}, u32[]{:S(2)}) async-start(bf16[64,4,384]{2,0,1:T(8,128)(2,1)} %bitcast.182), calls=%async_computation.9 | async-start | bytes 393216 | tf_op jit(solution)/shard_map/all_to_all | solution.py:198
  713.1 62.4 %collective-permute-start.37 = (bf16[48,1536]{1,0:T(8,128)(2,1)S(1)}, bf16[48,1536]{1,0:T(8,128)(2,1)S(1)}, u32[]{:S(2)}, u32[]{:S(2)}) collective-permute-start(bf16[48,1536]{1,0:T(8,128)(2,1)S(1)} %get-tuple-element.157), channel_id=1, source_target_pairs={{0,0},{16,1},{2,2},{18,3},{4,4},{20,5},{6,6},{22,7},{8,8},{24,9},{... | collective-permute-start | bytes 442376 | tf_op jit(solution)/shard_map/ppermute | solution.py:159
  730.1 45.4 %collective-permute-start.38 = (bf16[48,1536]{1,0:T(8,128)(2,1)S(1)}, bf16[48,1536]{1,0:T(8,128)(2,1)S(1)}, u32[]{:S(2)}, u32[]{:S(2)}) collective-permute-start(bf16[48,1536]{1,0:T(8,128)(2,1)S(1)} %get-tuple-element.158), channel_id=1, source_target_pairs={{1,0},{17,1},{3,2},{19,3},{5,4},{21,5},{7,6},{23,7},{9,8},{25,9},{... | collective-permute-start | bytes 442376 | tf_op jit(solution)/shard_map/ppermute | solution.py:160
  954.5 12.4 %collective-permute-start.36 = (bf16[192,384]{0,1:T(8,128)(2,1)S(1)}, bf16[192,384]{0,1:T(8,128)(2,1)S(1)}, u32[]{:S(2)}, u32[]{:S(2)}) collective-permute-start(bf16[192,384]{0,1:T(8,128)(2,1)S(1)} %broadcast_select_fusion.18), channel_id=1, source_target_pairs={{0,16},{8,24},{16,0},{24,8},{1,17},{9,25},{17,1},{25,9},{2,18},{10... | collective-permute-start | bytes 442376 | tf_op jit(solution)/shard_map/ppermute | solution.py:114
  955.8 6.6 collective-permute-start.35
  956.2 10.5 collective-permute-start.34
  1066.4 117.6 %collective-permute-start.39 = (bf16[192,1536]{1,0:T(8,128)(2,1)}, bf16[192,1536]{1,0:T(8,128)(2,1)}, u32[]{:S(2)}, u32[]{:S(2)}) collective-permute-start(bf16[192,1536]{1,0:T(8,128)(2,1)} %broadcast_select_fusion.8), channel_id=1, source_target_pairs={{0,16},{8,24},{16,0},{24,8},{1,17},{9,25},{17,1},{25,9},{2,18},{10... | collective-permute-start | bytes 1769480 | tf_op jit(solution)/shard_map/ppermute | solution.py:114
  1178.1 18.7 %collective-permute-start.40 = (bf16[192,1536]{1,0:T(8,128)(2,1)}, bf16[192,1536]{1,0:T(8,128)(2,1)S(1)}, u32[]{:S(2)}, u32[]{:S(2)}) collective-permute-start(bf16[192,1536]{1,0:T(8,128)(2,1)} %get-tuple-element.125), channel_id=1, source_target_pairs={{0,0},{16,1},{2,2},{18,3},{4,4},{20,5},{6,6},{22,7},{8,8},{24,9},{... | collective-permute-start | bytes 1769480 | tf_op jit(solution)/shard_map/ppermute | solution.py:159
  1183.9 14.2 %collective-permute-start.41 = (bf16[192,1536]{1,0:T(8,128)(2,1)}, bf16[192,1536]{1,0:T(8,128)(2,1)}, u32[]{:S(2)}, u32[]{:S(2)}) collective-permute-start(bf16[192,1536]{1,0:T(8,128)(2,1)} %get-tuple-element.126), channel_id=1, source_target_pairs={{1,0},{17,1},{3,2},{19,3},{5,4},{21,5},{7,6},{23,7},{9,8},{25,9},{... | collective-permute-start | bytes 1769480 | tf_op jit(solution)/shard_map/ppermute | solution.py:160
  (135 other events, 1757.0 us)
Sparse Core Ops, SparseCore 0:
  31.2 46.4 all-gather.4
  79.9 56.8 all-gather.6
  138.4 49.8 all-gather.8
  212.1 77.1 all-gather.10
  553.1 40.6 reduce-scatter.17
  633.7 39.0 reduce-scatter.15
  677.9 95.3 reduce-scatter.27
  776.4 87.8 all-reduce.1
  866.7 41.6 reduce-scatter.31
  910.6 42.2 reduce-scatter.29
  955.3 53.4 reduce-scatter.21
  1011.1 53.3 reduce-scatter.19
  1066.8 53.3 reduce-scatter.25
  1122.5 53.3 reduce-scatter.23
